TPU v7x, 512 devices: a whole 4x8x8 slice. The times are simulated.
512 devices in a mesh: gx: 32 (over z, x), gy: 16 (over y, core).
Axes of the slice: x: 4, y: 8, z: 8, core: 2. Of those that a mesh axis runs over, the one named last changes fastest.
Arguments:
- velocity_guess: float32 [8, 2, 1024, 4096], P(None, None, 'gx', 'gy'), may hold values from -6 to 6
- friction: bfloat16 [8, 1024, 4096], P(None, 'gx', 'gy'), may hold values from 0.5 to 4
- thickness: float32 [1024, 4096], P('gx', 'gy'), may hold values from 0.5 to 4.5
- surface: float32 [1024, 4096], P('gx', 'gy'), may hold values from -4 to 1284
- ice_mask: int32 [1024, 4096], P('gx', 'gy'), may hold values 0 or 1
- grounded_mask: int32 [1024, 4096], P('gx', 'gy'), may hold values 0 or 1
Outputs:
- velocity: float32 [8, 2, 1024, 4096], P(None, None, 'gx', 'gy')
All inputs are finite; a program needn't handle non-finite values. No bound on the sum of `ice_mask` or of `grounded_mask` on one device may be relied on, other than what follows from the above.
Results may differ from a plain program's by a relative error of at most 0.0003.
Values sent between devices are 32-bit elements; how exact they have to be, the bound alone decides.
A program may use at most 64 MiB of HBM per device.

v0:
```python
import jax
import jax.numpy as jnp
from jax import lax
from jax.sharding import PartitionSpec as P

strain_floor = 0.1
water_drag = 0.25
flow_power = 1.0 / 3.0


def padded_2(cells, sides, width):
    for axis, dim in sides:
        count = lax.axis_size(axis)
        ends = count - 1
        head = lax.slice_in_dim(cells, 0, width, axis=dim)
        tail = lax.slice_in_dim(cells, cells.shape[dim] - width, cells.shape[dim], axis=dim)
        cells = jnp.concatenate(
            [
                lax.ppermute(tail, axis, [(i, (i + 1) % count) for i in range(ends)]),
                cells,
                lax.ppermute(head, axis, [((i + 1) % count, i) for i in range(ends)]),
            ],
            axis=dim,
        )
    return cells


def centre_rows(padded):
    return 0.5 * (padded[..., 2:, 1:-1] - padded[..., :-2, 1:-1])


def centre_cols(padded):
    return 0.5 * (padded[..., 1:-1, 2:] - padded[..., 1:-1, :-2])


def strains(padded):
    field_u = padded[:, 0]
    field_v = padded[:, 1]
    return (centre_rows(field_u), centre_cols(field_v), centre_cols(field_u) + centre_rows(field_v))


def stresses(visc, padded):
    ka, kb, kc = strains(padded)
    return (visc * (4.0 * ka + 2.0 * kb), visc * (2.0 * ka + 4.0 * kb), visc * kc)


def divergence(sxx, syy, sxy, field, drag, icef):
    out_u = icef * (drag * field[:, 0] - centre_rows(sxx) - centre_cols(sxy))
    out_v = icef * (drag * field[:, 1] - centre_cols(syy) - centre_rows(sxy))
    return jnp.stack([out_u, out_v], 1)


def extend(field):
    flat = field.reshape((-1,) + field.shape[2:])
    grown = padded_2(flat, (("gx", 1), ("gy", 2)), 1)
    return grown.reshape(field.shape[:2] + grown.shape[1:])


def member_dot(left, right):
    return lax.psum(jnp.sum(left * right, axis=(1, 2, 3)), ("gx", "gy"))


def column(values):
    return values[:, None, None, None]


def per_device(velocity_guess, friction, thickness, surface, ice_mask, grounded_mask):
    members = velocity_guess.shape[0]
    icef = ice_mask.astype(jnp.float32)
    groundf = grounded_mask.astype(jnp.float32)
    drag = icef * (groundf * friction.astype(jnp.float32) + water_drag)
    start = icef * velocity_guess
    stacked = jnp.concatenate([start.reshape((-1,) + start.shape[2:]), surface[None]], 0)
    grown = padded_2(stacked, (("gx", 1), ("gy", 2)), 1)
    start_ext = grown[: 2 * members].reshape((members, 2) + grown.shape[1:])
    start_one = grown[: 2 * members].reshape((members, 2) + grown.shape[1:])
    surf_one = grown[2 * members]
    sa, sb, sc = strains(start_one)
    visc = (
        icef
        * 0.5
        * thickness
        * jnp.power(sa * sa + sb * sb + sa * sb + 0.25 * (sc * sc) + strain_floor, -flow_power)
    )
    visc_ext = padded_2(visc, (("gx", 1), ("gy", 2)), 1)
    near_rows = visc_ext[:, 2:, 1:-1] + visc_ext[:, :-2, 1:-1]
    near_cols = visc_ext[:, 1:-1, 2:] + visc_ext[:, 1:-1, :-2]
    precond = jnp.stack(
        [
            icef * (near_rows + 0.25 * near_cols + drag) + (1.0 - icef),
            icef * (near_cols + 0.25 * near_rows + drag) + (1.0 - icef),
        ],
        1,
    )
    force = jnp.stack(
        [icef * -(thickness * centre_rows(surf_one)), icef * -(thickness * centre_cols(surf_one))],
        0,
    )

    def operate(padded):
        sxx, syy, sxy = stresses(visc, padded)
        joined = jnp.concatenate([sxx, syy, sxy], 0)
        wider = padded_2(joined, (("gx", 1), ("gy", 2)), 1)
        field = padded[:, :, 1:-1, 1:-1]
        return divergence(
            wider[:members], wider[members : 2 * members], wider[2 * members :], field, drag, icef
        )

    velocity = start
    resid = force[None] - operate(start_ext)
    scaled = resid / precond
    direction = scaled
    norm_now = member_dot(resid, scaled)
    for step in range(2):
        image = operate(extend(direction))
        alpha = norm_now / member_dot(direction, image)
        velocity = velocity + column(alpha) * direction
        resid = resid - column(alpha) * image
        if step == 0:
            scaled = resid / precond
            norm_next = member_dot(resid, scaled)
            direction = scaled + column(norm_next / norm_now) * direction
            norm_now = norm_next
    return velocity


def solution(mesh):
    placed = (
        P(None, None, "gx", "gy"),
        P(None, "gx", "gy"),
        P("gx", "gy"),
        P("gx", "gy"),
        P("gx", "gy"),
        P("gx", "gy"),
    )
    return jax.shard_map(
        per_device, mesh=mesh, in_specs=placed, out_specs=P(None, None, "gx", "gy"), check_vma=False
    )
```

profile of v0, /device:TPU:10, one launch (start us, length us, event | category | flops | bytes accessed | tf_op | source)
XLA Modules:
  0.0 479.6 jit_solution(5027223697449381866)
XLA Ops:
  1.9 3.4 collective-permute-start
  7.8 3.2 collective-permute-done.1
  13.2 3.6 collective-permute-start.3
  26.6 3.4 collective-permute-start.9
  32.5 5.0 %collective-permute-start.5 = (f32[24,1,256]{2,1,0:T(1,128)S(1)}, f32[24,1,256]{2,1,0:T(1,128)S(1)}, u32[]{:S(2)}, u32[]{:S(2)}) collective-permute-start(f32[24,1,256]{2,1,0:T(1,128)S(1)} %get-tuple-element.38), channel_id=1, source_target_pairs={{0,16},{16,32},{32,48},{48,64},{64,80},{80,96},{96,112},{112,128},... | collective-permute-start | bytes 73736 | tf_op jit(solution)/shard_map/ppermute | solution.py:19
  37.7 3.4 collective-permute-start.10
  43.9 3.8 collective-permute-done.11
  53.1 3.8 collective-permute-done.6
  57.0 3.8 collective-permute-done.7
  61.8 5.8 %collective-permute-start.12 = (f32[16,1,256]{2,1,0:T(1,128)S(1)}, f32[16,1,256]{2,1,0:T(1,128)S(1)}, u32[]{:S(2)}, u32[]{:S(2)}) collective-permute-start(f32[16,1,256]{2,1,0:T(1,128)S(1)} %get-tuple-element.50), channel_id=1, source_target_pairs={{0,16},{16,32},{32,48},{48,64},{64,80},{80,96},{96,112},{112,128},... | collective-permute-start | bytes 49160 | tf_op jit(solution)/shard_map/ppermute | solution.py:19
  69.5 5.5 %collective-permute-done.13 = f32[16,1,256]{2,1,0:T(1,128)S(1)} collective-permute-done((f32[16,1,256]{2,1,0:T(1,128)S(1)}, f32[16,1,256]{2,1,0:T(1,128)S(1)}, u32[]{:S(2)}, u32[]{:S(2)}) %collective-permute-start.13) | collective-permute-done | bytes 16416 | tf_op jit(solution)/shard_map/ppermute | solution.py:21
  77.1 3.6 collective-permute-start.15
  88.5 3.9 collective-permute-start.17
  99.1 4.4 collective-permute-done.18
  103.5 3.8 collective-permute-done.19
  109.2 120.6 %all-reduce = (f32[8]{0:T(128)S(1)}, f32[8]{0:T(128)S(1)}) all-reduce(f32[8]{0:T(128)S(1)} %get-tuple-element.6, f32[8]{0:T(128)S(1)} %get-tuple-element.5), channel_id=1, replica_groups=mesh['gx'=32,'gy'=16] {'gx','gy'}, use_global_device_ids=true, to_apply=%region_1.0 | all-reduce | flops 16 | bytes 128 | tf_op jit(solution)/shard_map/psum | solution.py:60
  232.2 94.5 %psum.30 = f32[8]{0:T(128)S(1)} all-reduce(f32[8]{0:T(128)S(1)} %get-tuple-element.13), channel_id=1, replica_groups=mesh['gx'=32,'gy'=16] {'gx','gy'}, use_global_device_ids=true, to_apply=%region_5.0 | all-reduce | flops 8 | bytes 64 | tf_op jit(solution)/shard_map/psum | solution.py:60
  330.7 3.9 collective-permute-start.21
  338.5 3.8 collective-permute-start.23
  347.9 3.9 collective-permute-start.24
  353.7 3.8 collective-permute-done.25
  362.2 4.4 collective-permute-done.26
  366.6 3.8 collective-permute-done.27
  371.9 106.7 %psum.31 = f32[8]{0:T(128)S(1)} all-reduce(f32[8]{0:T(128)S(1)} %fusion), channel_id=1, replica_groups=mesh['gx'=32,'gy'=16] {'gx','gy'}, use_global_device_ids=true, to_apply=%region_7.0 | all-reduce | flops 8 | bytes 64 | tf_op jit(solution)/shard_map/psum | solution.py:60
  (132 shorter events, 72.9 us)
Async XLA Ops:
  1.9 5.9 %collective-permute-start = (f32[17,1,256]{2,1,0:T(1,128)S(1)}, f32[17,1,256]{2,1,0:T(1,128)S(1)}, u32[]{:S(2)}, u32[]{:S(2)}) collective-permute-start(f32[17,1,256]{2,1,0:T(1,128)S(1)} %get-tuple-element.45), channel_id=1, source_target_pairs={{0,16},{16,32},{32,48},{48,64},{64,80},{80,96},{96,112},{112,128},... | collective-permute-start | bytes 52232 | tf_op jit(solution)/shard_map/ppermute | solution.py:19
  11.2 8.6 %collective-permute-start.2 = (f32[17,34,1]{2,1,0:T(8,128)S(1)}, f32[17,34,1]{2,1,0:T(8,128)S(1)}, u32[]{:S(2)}, u32[]{:S(2)}) collective-permute-start(f32[17,34,1]{2,1,0:T(8,128)S(1)} %get-tuple-element.39), channel_id=1, source_target_pairs={{0,1},{1,2},{2,3},{3,4},{4,5},{5,6},{6,7},{7,8},{8,9},{9,10},{10,1... | collective-permute-start | bytes 6944 | tf_op jit(solution)/shard_map/ppermute | solution.py:19
  13.2 8.4 %collective-permute-start.3 = (f32[17,34,1]{2,1,0:T(8,128)S(1)}, f32[17,34,1]{2,1,0:T(8,128)S(1)}, u32[]{:S(2)}, u32[]{:S(2)}) collective-permute-start(f32[17,34,1]{2,1,0:T(8,128)S(1)} %get-tuple-element.40), channel_id=1, source_target_pairs={{1,0},{2,1},{3,2},{4,3},{5,4},{6,5},{7,6},{8,7},{9,8},{10,9},{11,1... | collective-permute-start | bytes 6944 | tf_op jit(solution)/shard_map/ppermute | solution.py:21
  24.2 13.3 %collective-permute-start.8 = (f32[8,1,256]{2,1,0:T(1,128)S(1)}, f32[8,1,256]{2,1,0:T(1,128)S(1)}, u32[]{:S(2)}, u32[]{:S(2)}) collective-permute-start(f32[8,1,256]{2,1,0:T(1,128)S(1)} %get-tuple-element.56), channel_id=1, source_target_pairs={{16,0},{32,16},{48,32},{64,48},{80,64},{96,80},{112,96},{128,112},... | collective-permute-start | bytes 24584 | tf_op jit(solution)/shard_map/ppermute | solution.py:21
  26.6 10.9 %collective-permute-start.9 = (f32[8,1,256]{2,1,0:T(1,128)S(1)}, f32[8,1,256]{2,1,0:T(1,128)S(1)}, u32[]{:S(2)}, u32[]{:S(2)}) collective-permute-start(f32[8,1,256]{2,1,0:T(1,128)S(1)} %get-tuple-element.57), channel_id=1, source_target_pairs={{0,16},{16,32},{32,48},{48,64},{64,80},{80,96},{96,112},{112,128},... | collective-permute-start | bytes 24584 | tf_op jit(solution)/shard_map/ppermute | solution.py:19
  30.1 18.3 %collective-permute-start.4 = (f32[24,1,256]{2,1,0:T(1,128)S(1)}, f32[24,1,256]{2,1,0:T(1,128)S(1)}, u32[]{:S(2)}, u32[]{:S(2)}) collective-permute-start(f32[24,1,256]{2,1,0:T(1,128)S(1)} %get-tuple-element.37), channel_id=1, source_target_pairs={{16,0},{32,16},{48,32},{64,48},{80,64},{96,80},{112,96},{128,112},... | collective-permute-start | bytes 73736 | tf_op jit(solution)/shard_map/ppermute | solution.py:21
  32.5 15.8 %collective-permute-start.5 = (f32[24,1,256]{2,1,0:T(1,128)S(1)}, f32[24,1,256]{2,1,0:T(1,128)S(1)}, u32[]{:S(2)}, u32[]{:S(2)}) collective-permute-start(f32[24,1,256]{2,1,0:T(1,128)S(1)} %get-tuple-element.38), channel_id=1, source_target_pairs={{0,16},{16,32},{32,48},{48,64},{64,80},{80,96},{96,112},{112,128},... | collective-permute-start | bytes 73736 | tf_op jit(solution)/shard_map/ppermute | solution.py:19
  37.7 6.2 %collective-permute-start.10 = (f32[8,34,1]{2,1,0:T(8,128)S(1)}, f32[8,34,1]{2,1,0:T(8,128)S(1)}, u32[]{:S(2)}, u32[]{:S(2)}) collective-permute-start(f32[8,34,1]{2,1,0:T(8,128)S(1)} %get-tuple-element.52), channel_id=1, source_target_pairs={{1,0},{2,1},{3,2},{4,3},{5,4},{6,5},{7,6},{8,7},{9,8},{10,9},{11,1... | collective-permute-start | bytes 3272 | tf_op jit(solution)/shard_map/ppermute | solution.py:21
  41.1 6.6 %collective-permute-start.11 = (f32[8,34,1]{2,1,0:T(8,128)S(1)}, f32[8,34,1]{2,1,0:T(8,128)S(1)}, u32[]{:S(2)}, u32[]{:S(2)}) collective-permute-start(f32[8,34,1]{2,1,0:T(8,128)S(1)} %get-tuple-element.53), channel_id=1, source_target_pairs={{0,1},{1,2},{2,3},{3,4},{4,5},{5,6},{6,7},{7,8},{8,9},{9,10},{10,1... | collective-permute-start | bytes 3272 | tf_op jit(solution)/shard_map/ppermute | solution.py:19
  48.7 8.3 %collective-permute-start.6 = (f32[24,34,1]{2,1,0:T(8,128)S(1)}, f32[24,34,1]{2,1,0:T(8,128)S(1)}, u32[]{:S(2)}, u32[]{:S(2)}) collective-permute-start(f32[24,34,1]{2,1,0:T(8,128)S(1)} %get-tuple-element.29), channel_id=1, source_target_pairs={{1,0},{2,1},{3,2},{4,3},{5,4},{6,5},{7,6},{8,7},{9,8},{10,9},{11,1... | collective-permute-start | bytes 9800 | tf_op jit(solution)/shard_map/ppermute | solution.py:21
  50.6 10.1 %collective-permute-start.7 = (f32[24,34,1]{2,1,0:T(8,128)S(1)}, f32[24,34,1]{2,1,0:T(8,128)S(1)}, u32[]{:S(2)}, u32[]{:S(2)}) collective-permute-start(f32[24,34,1]{2,1,0:T(8,128)S(1)} %get-tuple-element.30), channel_id=1, source_target_pairs={{0,1},{1,2},{2,3},{3,4},{4,5},{5,6},{6,7},{7,8},{8,9},{9,10},{10,1... | collective-permute-start | bytes 9800 | tf_op jit(solution)/shard_map/ppermute | solution.py:19
  61.8 7.7 %collective-permute-start.12 = (f32[16,1,256]{2,1,0:T(1,128)S(1)}, f32[16,1,256]{2,1,0:T(1,128)S(1)}, u32[]{:S(2)}, u32[]{:S(2)}) collective-permute-start(f32[16,1,256]{2,1,0:T(1,128)S(1)} %get-tuple-element.50), channel_id=1, source_target_pairs={{0,16},{16,32},{32,48},{48,64},{64,80},{80,96},{96,112},{112,128},... | collective-permute-start | bytes 49160 | tf_op jit(solution)/shard_map/ppermute | solution.py:19
  67.5 7.5 %collective-permute-start.13 = (f32[16,1,256]{2,1,0:T(1,128)S(1)}, f32[16,1,256]{2,1,0:T(1,128)S(1)}, u32[]{:S(2)}, u32[]{:S(2)}) collective-permute-start(f32[16,1,256]{2,1,0:T(1,128)S(1)} %get-tuple-element.51), channel_id=1, source_target_pairs={{16,0},{32,16},{48,32},{64,48},{80,64},{96,80},{112,96},{128,112},... | collective-permute-start | bytes 49160 | tf_op jit(solution)/shard_map/ppermute | solution.py:21
  75.2 8.4 %collective-permute-start.14 = (f32[16,34,1]{2,1,0:T(8,128)S(1)}, f32[16,34,1]{2,1,0:T(8,128)S(1)}, u32[]{:S(2)}, u32[]{:S(2)}) collective-permute-start(f32[16,34,1]{2,1,0:T(8,128)S(1)} %get-tuple-element.43), channel_id=1, source_target_pairs={{0,1},{1,2},{2,3},{3,4},{4,5},{5,6},{6,7},{7,8},{8,9},{9,10},{10,1... | collective-permute-start | bytes 6536 | tf_op jit(solution)/shard_map/ppermute | solution.py:19
  77.1 8.2 %collective-permute-start.15 = (f32[16,34,1]{2,1,0:T(8,128)S(1)}, f32[16,34,1]{2,1,0:T(8,128)S(1)}, u32[]{:S(2)}, u32[]{:S(2)}) collective-permute-start(f32[16,34,1]{2,1,0:T(8,128)S(1)} %get-tuple-element.44), channel_id=1, source_target_pairs={{1,0},{2,1},{3,2},{4,3},{5,4},{6,5},{7,6},{8,7},{9,8},{10,9},{11,1... | collective-permute-start | bytes 6536 | tf_op jit(solution)/shard_map/ppermute | solution.py:21
  86.5 5.9 %collective-permute-start.16 = (f32[24,1,256]{2,1,0:T(1,128)S(1)}, f32[24,1,256]{2,1,0:T(1,128)S(1)}, u32[]{:S(2)}, u32[]{:S(2)}) collective-permute-start(f32[24,1,256]{2,1,0:T(1,128)S(1)} %get-tuple-element.35), channel_id=1, source_target_pairs={{16,0},{32,16},{48,32},{64,48},{80,64},{96,80},{112,96},{128,112},... | collective-permute-start | bytes 73736 | tf_op jit(solution)/shard_map/ppermute | solution.py:21
  94.5 9.0 %collective-permute-start.18 = (f32[24,34,1]{2,1,0:T(8,128)S(1)}, f32[24,34,1]{2,1,0:T(8,128)S(1)}, u32[]{:S(2)}, u32[]{:S(2)}) collective-permute-start(f32[24,34,1]{2,1,0:T(8,128)S(1)} %get-tuple-element.25), channel_id=1, source_target_pairs={{1,0},{2,1},{3,2},{4,3},{5,4},{6,5},{7,6},{8,7},{9,8},{10,9},{11,1... | collective-permute-start | bytes 9800 | tf_op jit(solution)/shard_map/ppermute | solution.py:21
  97.2 10.1 %collective-permute-start.19 = (f32[24,34,1]{2,1,0:T(8,128)S(1)}, f32[24,34,1]{2,1,0:T(8,128)S(1)}, u32[]{:S(2)}, u32[]{:S(2)}) collective-permute-start(f32[24,34,1]{2,1,0:T(8,128)S(1)} %get-tuple-element.26), channel_id=1, source_target_pairs={{0,1},{1,2},{2,3},{3,4},{4,5},{5,6},{6,7},{7,8},{8,9},{9,10},{10,1... | collective-permute-start | bytes 9800 | tf_op jit(solution)/shard_map/ppermute | solution.py:19
  328.8 5.9 %collective-permute-start.20 = (f32[16,1,256]{2,1,0:T(1,128)S(1)}, f32[16,1,256]{2,1,0:T(1,128)S(1)}, u32[]{:S(2)}, u32[]{:S(2)}) collective-permute-start(f32[16,1,256]{2,1,0:T(1,128)S(1)} %get-tuple-element.48), channel_id=1, source_target_pairs={{0,16},{16,32},{32,48},{48,64},{64,80},{80,96},{96,112},{112,128},... | collective-permute-start | bytes 49160 | tf_op jit(solution)/shard_map/ppermute | solution.py:19
  336.6 8.4 %collective-permute-start.22 = (f32[16,34,1]{2,1,0:T(8,128)S(1)}, f32[16,34,1]{2,1,0:T(8,128)S(1)}, u32[]{:S(2)}, u32[]{:S(2)}) collective-permute-start(f32[16,34,1]{2,1,0:T(8,128)S(1)} %get-tuple-element.41), channel_id=1, source_target_pairs={{0,1},{1,2},{2,3},{3,4},{4,5},{5,6},{6,7},{7,8},{8,9},{9,10},{10,1... | collective-permute-start | bytes 6536 | tf_op jit(solution)/shard_map/ppermute | solution.py:19
  338.5 8.2 %collective-permute-start.23 = (f32[16,34,1]{2,1,0:T(8,128)S(1)}, f32[16,34,1]{2,1,0:T(8,128)S(1)}, u32[]{:S(2)}, u32[]{:S(2)}) collective-permute-start(f32[16,34,1]{2,1,0:T(8,128)S(1)} %get-tuple-element.42), channel_id=1, source_target_pairs={{1,0},{2,1},{3,2},{4,3},{5,4},{6,5},{7,6},{8,7},{9,8},{10,9},{11,1... | collective-permute-start | bytes 6536 | tf_op jit(solution)/shard_map/ppermute | solution.py:21
  347.9 5.9 %collective-permute-start.24 = (f32[24,1,256]{2,1,0:T(1,128)S(1)}, f32[24,1,256]{2,1,0:T(1,128)S(1)}, u32[]{:S(2)}, u32[]{:S(2)}) collective-permute-start(f32[24,1,256]{2,1,0:T(1,128)S(1)} %get-tuple-element.33), channel_id=1, source_target_pairs={{16,0},{32,16},{48,32},{64,48},{80,64},{96,80},{112,96},{128,112},... | collective-permute-start | bytes 73736 | tf_op jit(solution)/shard_map/ppermute | solution.py:21
  357.9 8.7 %collective-permute-start.26 = (f32[24,34,1]{2,1,0:T(8,128)S(1)}, f32[24,34,1]{2,1,0:T(8,128)S(1)}, u32[]{:S(2)}, u32[]{:S(2)}) collective-permute-start(f32[24,34,1]{2,1,0:T(8,128)S(1)} %get-tuple-element.21), channel_id=1, source_target_pairs={{1,0},{2,1},{3,2},{4,3},{5,4},{6,5},{7,6},{8,7},{9,8},{10,9},{11,1... | collective-permute-start | bytes 9800 | tf_op jit(solution)/shard_map/ppermute | solution.py:21
  360.3 10.1 %collective-permute-start.27 = (f32[24,34,1]{2,1,0:T(8,128)S(1)}, f32[24,34,1]{2,1,0:T(8,128)S(1)}, u32[]{:S(2)}, u32[]{:S(2)}) collective-permute-start(f32[24,34,1]{2,1,0:T(8,128)S(1)} %get-tuple-element.22), channel_id=1, source_target_pairs={{0,1},{1,2},{2,3},{3,4},{4,5},{5,6},{6,7},{7,8},{8,9},{9,10},{10,1... | collective-permute-start | bytes 9800 | tf_op jit(solution)/shard_map/ppermute | solution.py:19
  (21 other events, 653.1 us)
where the time goes:
time: 481 us; the launch traced here: 480 us
  blocking collectives  322 us (67%)
  starting transfers between devices  79.7 us (17%)
  waiting for transfers between devices  58.4 us (12%)
  other arithmetic  13.5 us (3%)
  local copies, waits for them, and re-layouts  5.37 us (1%)
    psum x3, blocking collectives, member_dot(): return lax.psum(jnp.sum(left * right, axis=(1, 2, 3)), ('gx', 'gy'))  322 us
    ppermute x14, starting transfers between devices, padded_2(): lax.ppermute(head, axis, [((i + 1) % count, i) for i in range(ends)])  40.5 us
    ppermute x14, starting transfers between devices, padded_2(): lax.ppermute(tail, axis, [(i, (i + 1) % count) for i in range(ends)])  39.2 us
    ppermute x14, waiting for transfers between devices, padded_2(): lax.ppermute(tail, axis, [(i, (i + 1) % count) for i in range(ends)])  29.3 us
    ppermute x14, waiting for transfers between devices, padded_2(): lax.ppermute(head, axis, [((i + 1) % count, i) for i in range(ends)])  29.1 us
  transfers between devices with their start and end apart: 28, of which 19 were waited for; matrix products, arithmetic and copies ran while one was open for 0% of the time, Pallas kernels for 0%

commit v1 on v0

--- a/solution.py
+++ b/solution.py
@@ -57,7 +57,7 @@
 
 
 def member_dot(left, right):
-    return lax.psum(jnp.sum(left * right, axis=(1, 2, 3)), ("gx", "gy"))
+    return jnp.sum(lax.all_gather(jnp.sum(left * right, axis=(1, 2, 3)), ("gx", "gy")), axis=0)
 
 
 def column(values):

time: 481 us -> 491 us (1.021)
    unnamed x0 -> x3, blocking collectives: none -> 322 us
    psum x3 -> x0, blocking collectives: 322 us -> none  [member_dot(): return lax.psum(jnp.sum(left * right, axis=(1, 2, 3)), ('gx', 'gy'))]
where the time goes in v1:
time: 491 us; the launch traced here: 489 us
  blocking collectives  322 us (66%)
  starting transfers between devices  79.5 us (16%)
  waiting for transfers between devices  59 us (12%)
  other arithmetic  17.3 us (4%)
  local copies, waits for them, and re-layouts  10.2 us (2%)
    unnamed x3, blocking collectives  322 us
    ppermute x14, starting transfers between devices, padded_2(): lax.ppermute(head, axis, [((i + 1) % count, i) for i in range(ends)])  40.3 us
    ppermute x14, starting transfers between devices, padded_2(): lax.ppermute(tail, axis, [(i, (i + 1) % count) for i in range(ends)])  39.2 us
    ppermute x14, waiting for transfers between devices, padded_2(): lax.ppermute(tail, axis, [(i, (i + 1) % count) for i in range(ends)])  29.5 us
    ppermute x14, waiting for transfers between devices, padded_2(): lax.ppermute(head, axis, [((i + 1) % count, i) for i in range(ends)])  29.5 us
  transfers between devices with their start and end apart: 28, of which 19 were waited for; matrix products, arithmetic and copies ran while one was open for 0% of the time, Pallas kernels for 0%

profile of v1, /device:TPU:10, one launch (start us, length us, event | category | flops | bytes accessed | tf_op | source)
XLA Modules:
  0.0 489.2 jit_solution(9402331727566752149)
XLA Ops:
  1.9 3.4 collective-permute-start
  7.8 3.2 collective-permute-done.1
  13.1 3.6 collective-permute-start.3
  26.6 3.4 collective-permute-start.9
  32.5 5.0 %collective-permute-start.5 = (f32[24,1,256]{2,1,0:T(1,128)S(1)}, f32[24,1,256]{2,1,0:T(1,128)S(1)}, u32[]{:S(2)}, u32[]{:S(2)}) collective-permute-start(f32[24,1,256]{2,1,0:T(1,128)S(1)} %get-tuple-element.38), channel_id=1, source_target_pairs={{0,16},{16,32},{32,48},{48,64},{64,80},{80,96},{96,112},{112,128},... | collective-permute-start | bytes 73736 | tf_op jit(solution)/shard_map/ppermute | solution.py:19
  37.6 3.4 collective-permute-start.10
  43.8 3.8 collective-permute-done.11
  53.1 3.8 collective-permute-done.6
  56.9 3.8 collective-permute-done.7
  62.4 5.8 %collective-permute-start.12 = (f32[16,1,256]{2,1,0:T(1,128)S(1)}, f32[16,1,256]{2,1,0:T(1,128)S(1)}, u32[]{:S(2)}, u32[]{:S(2)}) collective-permute-start(f32[16,1,256]{2,1,0:T(1,128)S(1)} %get-tuple-element.50), channel_id=1, source_target_pairs={{0,16},{16,32},{32,48},{48,64},{64,80},{80,96},{96,112},{112,128},... | collective-permute-start | bytes 49160 | tf_op jit(solution)/shard_map/ppermute | solution.py:19
  70.1 5.5 %collective-permute-done.13 = f32[16,1,256]{2,1,0:T(1,128)S(1)} collective-permute-done((f32[16,1,256]{2,1,0:T(1,128)S(1)}, f32[16,1,256]{2,1,0:T(1,128)S(1)}, u32[]{:S(2)}, u32[]{:S(2)}) %collective-permute-start.13) | collective-permute-done | bytes 16416 | tf_op jit(solution)/shard_map/ppermute | solution.py:21
  77.8 3.6 collective-permute-start.15
  90.0 3.9 collective-permute-start.17
  101.5 4.7 collective-permute-done.18
  106.2 3.8 collective-permute-done.19
  114.4 120.8 %all-reduce.4 = (f32[4096]{0:T(1024)S(1)}, f32[4096]{0:T(1024)S(1)}) all-reduce(f32[4096]{0:T(1024)S(1)} %dynamic-update-slice, f32[4096]{0:T(1024)S(1)} %dynamic-update-slice.1), channel_id=2, replica_groups=mesh['gx'=32,'gy'=16] {'gx','gy'}, use_global_device_ids=true, to_apply=%add | all-reduce | flops 8192 | bytes 65536
  239.0 94.7 %all-reduce.2 = f32[4096]{0:T(1024)S(1)} all-reduce(f32[4096]{0:T(1024)S(1)} %dynamic-update-slice.2), channel_id=4, replica_groups=mesh['gx'=32,'gy'=16] {'gx','gy'}, use_global_device_ids=true, to_apply=%add.2 | all-reduce | flops 4096 | bytes 32768
  339.5 3.9 collective-permute-start.21
  347.3 3.6 collective-permute-start.23
  356.6 3.9 collective-permute-start.24
  362.5 3.8 collective-permute-done.25
  371.0 4.4 collective-permute-done.26
  375.3 3.8 collective-permute-done.27
  381.1 106.8 %all-reduce.3 = f32[4096]{0:T(1024)S(1)} all-reduce(f32[4096]{0:T(1024)S(1)} %dynamic-update-slice.3), channel_id=5, replica_groups=mesh['gx'=32,'gy'=16] {'gx','gy'}, use_global_device_ids=true, to_apply=%add.3 | all-reduce | flops 4096 | bytes 32768
  (144 shorter events, 81.8 us)
Async XLA Ops:
  1.9 5.9 %collective-permute-start = (f32[17,1,256]{2,1,0:T(1,128)S(1)}, f32[17,1,256]{2,1,0:T(1,128)S(1)}, u32[]{:S(2)}, u32[]{:S(2)}) collective-permute-start(f32[17,1,256]{2,1,0:T(1,128)S(1)} %get-tuple-element.45), channel_id=1, source_target_pairs={{0,16},{16,32},{32,48},{48,64},{64,80},{80,96},{96,112},{112,128},... | collective-permute-start | bytes 52232 | tf_op jit(solution)/shard_map/ppermute | solution.py:19
  11.2 8.6 %collective-permute-start.2 = (f32[17,34,1]{2,1,0:T(8,128)S(1)}, f32[17,34,1]{2,1,0:T(8,128)S(1)}, u32[]{:S(2)}, u32[]{:S(2)}) collective-permute-start(f32[17,34,1]{2,1,0:T(8,128)S(1)} %get-tuple-element.39), channel_id=1, source_target_pairs={{0,1},{1,2},{2,3},{3,4},{4,5},{5,6},{6,7},{7,8},{8,9},{9,10},{10,1... | collective-permute-start | bytes 6944 | tf_op jit(solution)/shard_map/ppermute | solution.py:19
  13.1 8.4 %collective-permute-start.3 = (f32[17,34,1]{2,1,0:T(8,128)S(1)}, f32[17,34,1]{2,1,0:T(8,128)S(1)}, u32[]{:S(2)}, u32[]{:S(2)}) collective-permute-start(f32[17,34,1]{2,1,0:T(8,128)S(1)} %get-tuple-element.40), channel_id=1, source_target_pairs={{1,0},{2,1},{3,2},{4,3},{5,4},{6,5},{7,6},{8,7},{9,8},{10,9},{11,1... | collective-permute-start | bytes 6944 | tf_op jit(solution)/shard_map/ppermute | solution.py:21
  24.1 13.3 %collective-permute-start.8 = (f32[8,1,256]{2,1,0:T(1,128)S(1)}, f32[8,1,256]{2,1,0:T(1,128)S(1)}, u32[]{:S(2)}, u32[]{:S(2)}) collective-permute-start(f32[8,1,256]{2,1,0:T(1,128)S(1)} %get-tuple-element.56), channel_id=1, source_target_pairs={{16,0},{32,16},{48,32},{64,48},{80,64},{96,80},{112,96},{128,112},... | collective-permute-start | bytes 24584 | tf_op jit(solution)/shard_map/ppermute | solution.py:21
  26.6 10.9 %collective-permute-start.9 = (f32[8,1,256]{2,1,0:T(1,128)S(1)}, f32[8,1,256]{2,1,0:T(1,128)S(1)}, u32[]{:S(2)}, u32[]{:S(2)}) collective-permute-start(f32[8,1,256]{2,1,0:T(1,128)S(1)} %get-tuple-element.57), channel_id=1, source_target_pairs={{0,16},{16,32},{32,48},{48,64},{64,80},{80,96},{96,112},{112,128},... | collective-permute-start | bytes 24584 | tf_op jit(solution)/shard_map/ppermute | solution.py:19
  30.0 18.3 %collective-permute-start.4 = (f32[24,1,256]{2,1,0:T(1,128)S(1)}, f32[24,1,256]{2,1,0:T(1,128)S(1)}, u32[]{:S(2)}, u32[]{:S(2)}) collective-permute-start(f32[24,1,256]{2,1,0:T(1,128)S(1)} %get-tuple-element.37), channel_id=1, source_target_pairs={{16,0},{32,16},{48,32},{64,48},{80,64},{96,80},{112,96},{128,112},... | collective-permute-start | bytes 73736 | tf_op jit(solution)/shard_map/ppermute | solution.py:21
  32.5 15.8 %collective-permute-start.5 = (f32[24,1,256]{2,1,0:T(1,128)S(1)}, f32[24,1,256]{2,1,0:T(1,128)S(1)}, u32[]{:S(2)}, u32[]{:S(2)}) collective-permute-start(f32[24,1,256]{2,1,0:T(1,128)S(1)} %get-tuple-element.38), channel_id=1, source_target_pairs={{0,16},{16,32},{32,48},{48,64},{64,80},{80,96},{96,112},{112,128},... | collective-permute-start | bytes 73736 | tf_op jit(solution)/shard_map/ppermute | solution.py:19
  37.6 6.2 %collective-permute-start.10 = (f32[8,34,1]{2,1,0:T(8,128)S(1)}, f32[8,34,1]{2,1,0:T(8,128)S(1)}, u32[]{:S(2)}, u32[]{:S(2)}) collective-permute-start(f32[8,34,1]{2,1,0:T(8,128)S(1)} %get-tuple-element.52), channel_id=1, source_target_pairs={{1,0},{2,1},{3,2},{4,3},{5,4},{6,5},{7,6},{8,7},{9,8},{10,9},{11,1... | collective-permute-start | bytes 3272 | tf_op jit(solution)/shard_map/ppermute | solution.py:21
  41.0 6.6 %collective-permute-start.11 = (f32[8,34,1]{2,1,0:T(8,128)S(1)}, f32[8,34,1]{2,1,0:T(8,128)S(1)}, u32[]{:S(2)}, u32[]{:S(2)}) collective-permute-start(f32[8,34,1]{2,1,0:T(8,128)S(1)} %get-tuple-element.53), channel_id=1, source_target_pairs={{0,1},{1,2},{2,3},{3,4},{4,5},{5,6},{6,7},{7,8},{8,9},{9,10},{10,1... | collective-permute-start | bytes 3272 | tf_op jit(solution)/shard_map/ppermute | solution.py:19
  48.6 8.3 %collective-permute-start.6 = (f32[24,34,1]{2,1,0:T(8,128)S(1)}, f32[24,34,1]{2,1,0:T(8,128)S(1)}, u32[]{:S(2)}, u32[]{:S(2)}) collective-permute-start(f32[24,34,1]{2,1,0:T(8,128)S(1)} %get-tuple-element.29), channel_id=1, source_target_pairs={{1,0},{2,1},{3,2},{4,3},{5,4},{6,5},{7,6},{8,7},{9,8},{10,9},{11,1... | collective-permute-start | bytes 9800 | tf_op jit(solution)/shard_map/ppermute | solution.py:21
  50.6 10.1 %collective-permute-start.7 = (f32[24,34,1]{2,1,0:T(8,128)S(1)}, f32[24,34,1]{2,1,0:T(8,128)S(1)}, u32[]{:S(2)}, u32[]{:S(2)}) collective-permute-start(f32[24,34,1]{2,1,0:T(8,128)S(1)} %get-tuple-element.30), channel_id=1, source_target_pairs={{0,1},{1,2},{2,3},{3,4},{4,5},{5,6},{6,7},{7,8},{8,9},{9,10},{10,1... | collective-permute-start | bytes 9800 | tf_op jit(solution)/shard_map/ppermute | solution.py:19
  62.4 7.7 %collective-permute-start.12 = (f32[16,1,256]{2,1,0:T(1,128)S(1)}, f32[16,1,256]{2,1,0:T(1,128)S(1)}, u32[]{:S(2)}, u32[]{:S(2)}) collective-permute-start(f32[16,1,256]{2,1,0:T(1,128)S(1)} %get-tuple-element.50), channel_id=1, source_target_pairs={{0,16},{16,32},{32,48},{48,64},{64,80},{80,96},{96,112},{112,128},... | collective-permute-start | bytes 49160 | tf_op jit(solution)/shard_map/ppermute | solution.py:19
  68.2 7.5 %collective-permute-start.13 = (f32[16,1,256]{2,1,0:T(1,128)S(1)}, f32[16,1,256]{2,1,0:T(1,128)S(1)}, u32[]{:S(2)}, u32[]{:S(2)}) collective-permute-start(f32[16,1,256]{2,1,0:T(1,128)S(1)} %get-tuple-element.51), channel_id=1, source_target_pairs={{16,0},{32,16},{48,32},{64,48},{80,64},{96,80},{112,96},{128,112},... | collective-permute-start | bytes 49160 | tf_op jit(solution)/shard_map/ppermute | solution.py:21
  75.9 8.4 %collective-permute-start.14 = (f32[16,34,1]{2,1,0:T(8,128)S(1)}, f32[16,34,1]{2,1,0:T(8,128)S(1)}, u32[]{:S(2)}, u32[]{:S(2)}) collective-permute-start(f32[16,34,1]{2,1,0:T(8,128)S(1)} %get-tuple-element.43), channel_id=1, source_target_pairs={{0,1},{1,2},{2,3},{3,4},{4,5},{5,6},{6,7},{7,8},{8,9},{9,10},{10,1... | collective-permute-start | bytes 6536 | tf_op jit(solution)/shard_map/ppermute | solution.py:19
  77.8 8.2 %collective-permute-start.15 = (f32[16,34,1]{2,1,0:T(8,128)S(1)}, f32[16,34,1]{2,1,0:T(8,128)S(1)}, u32[]{:S(2)}, u32[]{:S(2)}) collective-permute-start(f32[16,34,1]{2,1,0:T(8,128)S(1)} %get-tuple-element.44), channel_id=1, source_target_pairs={{1,0},{2,1},{3,2},{4,3},{5,4},{6,5},{7,6},{8,7},{9,8},{10,9},{11,1... | collective-permute-start | bytes 6536 | tf_op jit(solution)/shard_map/ppermute | solution.py:21
  88.1 5.9 %collective-permute-start.16 = (f32[24,1,256]{2,1,0:T(1,128)S(1)}, f32[24,1,256]{2,1,0:T(1,128)S(1)}, u32[]{:S(2)}, u32[]{:S(2)}) collective-permute-start(f32[24,1,256]{2,1,0:T(1,128)S(1)} %get-tuple-element.35), channel_id=1, source_target_pairs={{16,0},{32,16},{48,32},{64,48},{80,64},{96,80},{112,96},{128,112},... | collective-permute-start | bytes 73736 | tf_op jit(solution)/shard_map/ppermute | solution.py:21
  96.9 9.3 %collective-permute-start.18 = (f32[24,34,1]{2,1,0:T(8,128)}, f32[24,34,1]{2,1,0:T(8,128)}, u32[]{:S(2)}, u32[]{:S(2)}) collective-permute-start(f32[24,34,1]{2,1,0:T(8,128)} %get-tuple-element.25), channel_id=1, source_target_pairs={{1,0},{2,1},{3,2},{4,3},{5,4},{6,5},{7,6},{8,7},{9,8},{10,9},{11,1... | collective-permute-start | bytes 9800 | tf_op jit(solution)/shard_map/ppermute | solution.py:21
  99.6 10.5 %collective-permute-start.19 = (f32[24,34,1]{2,1,0:T(8,128)}, f32[24,34,1]{2,1,0:T(8,128)}, u32[]{:S(2)}, u32[]{:S(2)}) collective-permute-start(f32[24,34,1]{2,1,0:T(8,128)} %get-tuple-element.26), channel_id=1, source_target_pairs={{0,1},{1,2},{2,3},{3,4},{4,5},{5,6},{6,7},{7,8},{8,9},{9,10},{10,1... | collective-permute-start | bytes 9800 | tf_op jit(solution)/shard_map/ppermute | solution.py:19
  337.5 5.9 %collective-permute-start.20 = (f32[16,1,256]{2,1,0:T(1,128)S(1)}, f32[16,1,256]{2,1,0:T(1,128)S(1)}, u32[]{:S(2)}, u32[]{:S(2)}) collective-permute-start(f32[16,1,256]{2,1,0:T(1,128)S(1)} %get-tuple-element.48), channel_id=1, source_target_pairs={{0,16},{16,32},{32,48},{48,64},{64,80},{80,96},{96,112},{112,128},... | collective-permute-start | bytes 49160 | tf_op jit(solution)/shard_map/ppermute | solution.py:19
  345.3 8.4 %collective-permute-start.22 = (f32[16,34,1]{2,1,0:T(8,128)S(1)}, f32[16,34,1]{2,1,0:T(8,128)S(1)}, u32[]{:S(2)}, u32[]{:S(2)}) collective-permute-start(f32[16,34,1]{2,1,0:T(8,128)S(1)} %get-tuple-element.41), channel_id=1, source_target_pairs={{0,1},{1,2},{2,3},{3,4},{4,5},{5,6},{6,7},{7,8},{8,9},{9,10},{10,1... | collective-permute-start | bytes 6536 | tf_op jit(solution)/shard_map/ppermute | solution.py:19
  347.3 8.2 %collective-permute-start.23 = (f32[16,34,1]{2,1,0:T(8,128)S(1)}, f32[16,34,1]{2,1,0:T(8,128)S(1)}, u32[]{:S(2)}, u32[]{:S(2)}) collective-permute-start(f32[16,34,1]{2,1,0:T(8,128)S(1)} %get-tuple-element.42), channel_id=1, source_target_pairs={{1,0},{2,1},{3,2},{4,3},{5,4},{6,5},{7,6},{8,7},{9,8},{10,9},{11,1... | collective-permute-start | bytes 6536 | tf_op jit(solution)/shard_map/ppermute | solution.py:21
  356.6 5.9 %collective-permute-start.24 = (f32[24,1,256]{2,1,0:T(1,128)S(1)}, f32[24,1,256]{2,1,0:T(1,128)S(1)}, u32[]{:S(2)}, u32[]{:S(2)}) collective-permute-start(f32[24,1,256]{2,1,0:T(1,128)S(1)} %get-tuple-element.33), channel_id=1, source_target_pairs={{16,0},{32,16},{48,32},{64,48},{80,64},{96,80},{112,96},{128,112},... | collective-permute-start | bytes 73736 | tf_op jit(solution)/shard_map/ppermute | solution.py:21
  366.6 8.7 %collective-permute-start.26 = (f32[24,34,1]{2,1,0:T(8,128)S(1)}, f32[24,34,1]{2,1,0:T(8,128)S(1)}, u32[]{:S(2)}, u32[]{:S(2)}) collective-permute-start(f32[24,34,1]{2,1,0:T(8,128)S(1)} %get-tuple-element.21), channel_id=1, source_target_pairs={{1,0},{2,1},{3,2},{4,3},{5,4},{6,5},{7,6},{8,7},{9,8},{10,9},{11,1... | collective-permute-start | bytes 9800 | tf_op jit(solution)/shard_map/ppermute | solution.py:21
  369.0 10.1 %collective-permute-start.27 = (f32[24,34,1]{2,1,0:T(8,128)S(1)}, f32[24,34,1]{2,1,0:T(8,128)S(1)}, u32[]{:S(2)}, u32[]{:S(2)}) collective-permute-start(f32[24,34,1]{2,1,0:T(8,128)S(1)} %get-tuple-element.22), channel_id=1, source_target_pairs={{0,1},{1,2},{2,3},{3,4},{4,5},{5,6},{6,7},{7,8},{8,9},{9,10},{10,1... | collective-permute-start | bytes 9800 | tf_op jit(solution)/shard_map/ppermute | solution.py:19
  (19 other events, 265.7 us)
